TPU v7x, 32 devices: a whole 2x2x4 slice. The times are simulated.
32 devices in a mesh: parts: 2 (over y), off: 4 (over z), depth: 2 (over x), shot: 2 (over core).
Axes of the slice: x: 2, y: 2, z: 4, core: 2. Of those that a mesh axis runs over, the one named last changes fastest.
Arguments:
- image: bfloat16 [64, 32, 32, 256], P('off', None, 'depth'), may hold values from -4 to 4
- offset_of: int32 [64], P('off'), may hold values from 0 to 63, each once
- background: bfloat16 [4, 32, 32, 256], P(('parts', 'shot'), 'off', 'depth'), parts along dimension 0, may hold values from -6 to 6
- wave_now: float32 [4, 32, 32, 256], P(('parts', 'shot'), 'off', 'depth'), parts along dimension 0, may hold values from -6 to 6
- wave_prev: float32 [4, 32, 32, 256], P(('parts', 'shot'), 'off', 'depth'), parts along dimension 0, may hold values from -6 to 6
- courant: float32 [32, 32, 256], P('off', 'depth'), may hold values from 0.02 to 0.15
Outputs:
- wave_next: float32 [4, 32, 32, 256], P(('parts', 'shot'), 'off', 'depth'), parts along dimension 0
There are 2 independent parts, one for each index of `parts`. A program takes and returns all parts, laid end to end along the dimension named above; an argument that names none is the same for every part. Nothing has to cross between parts.
Inputs may be any that keep to these rules, and one draw needn't show every extreme that they name: Each value appears once; image column k holds offset offset_of[k] - 32 cells along x.
All inputs are finite; a program needn't handle non-finite values.
Results may differ from a plain program's by a relative error of at most 0.0003.
Values may be sent and summed in bfloat16 or wider, within the bound.
A program may use at most 64 MiB of HBM per device.

v0:
```python
import jax
import jax.numpy as jnp
from jax import lax
from jax.sharding import PartitionSpec as P

H = 64
STENCIL = (-205.0 / 72.0, 8.0 / 5.0, -1.0 / 5.0, 8.0 / 315.0, -1.0 / 560.0)


def extended_2(cells, sides, width):
    for axis, dim in sides:
        count = lax.axis_size(axis)
        ends = count - 1
        head = lax.slice_in_dim(cells, 0, width, axis=dim)
        tail = lax.slice_in_dim(cells, cells.shape[dim] - width, cells.shape[dim], axis=dim)
        cells = jnp.concatenate(
            [
                lax.ppermute(tail, axis, [(i, (i + 1) % count) for i in range(ends)]),
                cells,
                lax.ppermute(head, axis, [((i + 1) % count, i) for i in range(ends)]),
            ],
            axis=dim,
        )
    return cells


def laplace(padded, rows_y, rows_z, cols_x):
    extended = jnp.pad(padded, ((0, 0), (0, 0), (4, 4)))
    centre = extended[4 : 4 + rows_y, 4 : 4 + rows_z, 4 : 4 + cols_x]
    running = 3.0 * STENCIL[0] * centre
    for radius in range(1, 5):
        beside_all = extended[4 + radius : 4 + radius + rows_y, 4 : 4 + rows_z, 4 : 4 + cols_x]
        beside_all = (
            beside_all + extended[4 - radius : 4 - radius + rows_y, 4 : 4 + rows_z, 4 : 4 + cols_x]
        )
        beside_all = (
            beside_all + extended[4 : 4 + rows_y, 4 + radius : 4 + radius + rows_z, 4 : 4 + cols_x]
        )
        beside_all = (
            beside_all + extended[4 : 4 + rows_y, 4 - radius : 4 - radius + rows_z, 4 : 4 + cols_x]
        )
        beside_all = (
            beside_all + extended[4 : 4 + rows_y, 4 : 4 + rows_z, 4 + radius : 4 + radius + cols_x]
        )
        beside_all = (
            beside_all + extended[4 : 4 + rows_y, 4 : 4 + rows_z, 4 - radius : 4 - radius + cols_x]
        )
        running = running + STENCIL[radius] * beside_all
    return running


def on_device(image, offset_of, background, wave_now, wave_prev, courant):
    slab_rows = wave_now.shape[1]
    depth_rows = wave_now.shape[2]
    width_x = wave_now.shape[3]
    local_cols = image.shape[0]
    half_span = H // 2
    gathered = lax.all_gather(background, "off", axis=1, tiled=True)
    extended_bg = jnp.pad(gathered[0], ((0, 0), (0, 0), (half_span, half_span)))
    first_index = jnp.asarray(jnp.int32(0), jnp.int32)

    def add_column(column, running):
        offset_cells = offset_of[column] - half_span
        whole_col = lax.dynamic_index_in_dim(image, column, 0, keepdims=False)
        starts = (first_index, jnp.zeros((), jnp.int32), half_span - offset_cells)
        shifted = lax.dynamic_slice(
            extended_bg, starts, (slab_rows * lax.axis_size("off"), depth_rows, width_x)
        )
        return running + whole_col.astype(jnp.float32) * shifted.astype(jnp.float32)

    own_source = lax.psum_scatter(
        lax.fori_loop(
            0,
            local_cols,
            add_column,
            jnp.zeros((slab_rows * lax.axis_size("off"), depth_rows, width_x), jnp.float32),
        ),
        "off",
        scatter_dimension=0,
        tiled=True,
    )
    padded = extended_2(wave_now[0], (("off", 0), ("depth", 1)), 4)
    bending = laplace(padded, slab_rows, depth_rows, width_x)
    stepped = 2.0 * wave_now[0] - wave_prev[0] + courant * (bending + own_source)
    return stepped[None]


def solution(mesh):
    return jax.shard_map(
        on_device,
        mesh=mesh,
        in_specs=(
            P("off", None, "depth", None),
            P("off"),
            P(("parts", "shot"), "off", "depth", None),
            P(("parts", "shot"), "off", "depth", None),
            P(("parts", "shot"), "off", "depth", None),
            P("off", "depth", None),
        ),
        out_specs=P(("parts", "shot"), "off", "depth", None),
        check_vma=False,
    )
```

profile of v0, /device:TPU:0, one launch (start us, length us, event | category | flops | bytes accessed | tf_op | source)
XLA Modules:
  0.0 105.7 jit_solution(5302099178217128605)
XLA Ops:
  6.5 15.9 %all_gather.3 = bf16[1,32,16,256]{3,2,0,1:T(8,128)(2,1)S(1)} all-gather(bf16[1,8,16,256]{3,2,0,1:T(8,128)(2,1)} %bitcast.29), channel_id=1, replica_groups=mesh['parts'=2,'off'=4,'depth'=2,'shot'=2] {'off'}, dimensions={1}, use_global_device_ids=true | all-gather | bytes 327680 | tf_op jit(solution)/shard_map/all_gather | solution.py:58
  22.6 50.0 %while.16 = (s32[]{:T(128)}, f32[32,16,256]{2,1,0:T(8,128)S(1)}, bf16[16,32,16,256]{3,2,1,0:T(8,128)(2,1)}, s32[16]{0:T(128)}, bf16[32,16,320]{2,1,0:T(8,128)(2,...) while((s32[]{:T(128)}, f32[32,16,256]{2,1,0:T(8,128)S(1)}, ...), condition=%wide.region_1.2_spmd.clone, body=%wide.region_0.1_spmd.clone.sunk | while | flops 655368 | bytes 1573061 | solution.py:72
  22.7 1.3 %dynamic_slice.41 = s32[1]{0:T(128)} dynamic-slice(s32[16]{0:T(128)} %get-tuple-element.227, s32[]{:T(128)S(6)} %copy.10), dynamic_slice_sizes={1} | dynamic-slice | bytes 12 | tf_op jit(solution)/shard_map/while/body/eval_jaxpr/dynamic_slice | solution.py:63
  24.6 1.2 %fusion.37 = f32[32,16,256]{2,1,0:T(8,128)S(1)} fusion(f32[32,16,256]{2,1,0:T(8,128)S(1)} %get-tuple-element.215, bf16[32,16,320]{2,1,0:T(8,128)(2,1)S(1)} %get-tuple-element.228, s32[]{:T(128)S(6)} %select_n.22, bf16[16,32,16,256]{3,2,1,0:T(8,128)(2,1)} %get-tuple-element.226, s32[]{:T(128)S(6)} %copy.10, pred[]{:T(512)S(6)} %compare.23), kind=kLoop, calls=%fused_computation.1.clone.1 | loop fusion | flops 655360 | bytes 1572873 | tf_op jit(solution)/shard_map/while/body/eval_jaxpr/add | solution.py:69
  25.9 1.3 %dynamic_slice.41 = s32[1]{0:T(128)} dynamic-slice(s32[16]{0:T(128)} %get-tuple-element.227, s32[]{:T(128)S(6)} %copy.10), dynamic_slice_sizes={1} | dynamic-slice | bytes 12 | tf_op jit(solution)/shard_map/while/body/eval_jaxpr/dynamic_slice | solution.py:63
  27.8 1.2 %fusion.37 = f32[32,16,256]{2,1,0:T(8,128)S(1)} fusion(f32[32,16,256]{2,1,0:T(8,128)S(1)} %get-tuple-element.215, bf16[32,16,320]{2,1,0:T(8,128)(2,1)S(1)} %get-tuple-element.228, s32[]{:T(128)S(6)} %select_n.22, bf16[16,32,16,256]{3,2,1,0:T(8,128)(2,1)} %get-tuple-element.226, s32[]{:T(128)S(6)} %copy.10, pred[]{:T(512)S(6)} %compare.23), kind=kLoop, calls=%fused_computation.1.clone.1 | loop fusion | flops 655360 | bytes 1572873 | tf_op jit(solution)/shard_map/while/body/eval_jaxpr/add | solution.py:69
  29.0 1.3 %dynamic_slice.41 = s32[1]{0:T(128)} dynamic-slice(s32[16]{0:T(128)} %get-tuple-element.227, s32[]{:T(128)S(6)} %copy.10), dynamic_slice_sizes={1} | dynamic-slice | bytes 12 | tf_op jit(solution)/shard_map/while/body/eval_jaxpr/dynamic_slice | solution.py:63
  30.9 1.2 %fusion.37 = f32[32,16,256]{2,1,0:T(8,128)S(1)} fusion(f32[32,16,256]{2,1,0:T(8,128)S(1)} %get-tuple-element.215, bf16[32,16,320]{2,1,0:T(8,128)(2,1)S(1)} %get-tuple-element.228, s32[]{:T(128)S(6)} %select_n.22, bf16[16,32,16,256]{3,2,1,0:T(8,128)(2,1)} %get-tuple-element.226, s32[]{:T(128)S(6)} %copy.10, pred[]{:T(512)S(6)} %compare.23), kind=kLoop, calls=%fused_computation.1.clone.1 | loop fusion | flops 655360 | bytes 1572873 | tf_op jit(solution)/shard_map/while/body/eval_jaxpr/add | solution.py:69
  32.1 1.3 %dynamic_slice.41 = s32[1]{0:T(128)} dynamic-slice(s32[16]{0:T(128)} %get-tuple-element.227, s32[]{:T(128)S(6)} %copy.10), dynamic_slice_sizes={1} | dynamic-slice | bytes 12 | tf_op jit(solution)/shard_map/while/body/eval_jaxpr/dynamic_slice | solution.py:63
  34.0 1.2 %fusion.37 = f32[32,16,256]{2,1,0:T(8,128)S(1)} fusion(f32[32,16,256]{2,1,0:T(8,128)S(1)} %get-tuple-element.215, bf16[32,16,320]{2,1,0:T(8,128)(2,1)S(1)} %get-tuple-element.228, s32[]{:T(128)S(6)} %select_n.22, bf16[16,32,16,256]{3,2,1,0:T(8,128)(2,1)} %get-tuple-element.226, s32[]{:T(128)S(6)} %copy.10, pred[]{:T(512)S(6)} %compare.23), kind=kLoop, calls=%fused_computation.1.clone.1 | loop fusion | flops 655360 | bytes 1572873 | tf_op jit(solution)/shard_map/while/body/eval_jaxpr/add | solution.py:69
  35.2 1.3 %dynamic_slice.41 = s32[1]{0:T(128)} dynamic-slice(s32[16]{0:T(128)} %get-tuple-element.227, s32[]{:T(128)S(6)} %copy.10), dynamic_slice_sizes={1} | dynamic-slice | bytes 12 | tf_op jit(solution)/shard_map/while/body/eval_jaxpr/dynamic_slice | solution.py:63
  37.1 1.2 %fusion.37 = f32[32,16,256]{2,1,0:T(8,128)S(1)} fusion(f32[32,16,256]{2,1,0:T(8,128)S(1)} %get-tuple-element.215, bf16[32,16,320]{2,1,0:T(8,128)(2,1)S(1)} %get-tuple-element.228, s32[]{:T(128)S(6)} %select_n.22, bf16[16,32,16,256]{3,2,1,0:T(8,128)(2,1)} %get-tuple-element.226, s32[]{:T(128)S(6)} %copy.10, pred[]{:T(512)S(6)} %compare.23), kind=kLoop, calls=%fused_computation.1.clone.1 | loop fusion | flops 655360 | bytes 1572873 | tf_op jit(solution)/shard_map/while/body/eval_jaxpr/add | solution.py:69
  38.3 1.3 %dynamic_slice.41 = s32[1]{0:T(128)} dynamic-slice(s32[16]{0:T(128)} %get-tuple-element.227, s32[]{:T(128)S(6)} %copy.10), dynamic_slice_sizes={1} | dynamic-slice | bytes 12 | tf_op jit(solution)/shard_map/while/body/eval_jaxpr/dynamic_slice | solution.py:63
  40.2 1.2 %fusion.37 = f32[32,16,256]{2,1,0:T(8,128)S(1)} fusion(f32[32,16,256]{2,1,0:T(8,128)S(1)} %get-tuple-element.215, bf16[32,16,320]{2,1,0:T(8,128)(2,1)S(1)} %get-tuple-element.228, s32[]{:T(128)S(6)} %select_n.22, bf16[16,32,16,256]{3,2,1,0:T(8,128)(2,1)} %get-tuple-element.226, s32[]{:T(128)S(6)} %copy.10, pred[]{:T(512)S(6)} %compare.23), kind=kLoop, calls=%fused_computation.1.clone.1 | loop fusion | flops 655360 | bytes 1572873 | tf_op jit(solution)/shard_map/while/body/eval_jaxpr/add | solution.py:69
  41.4 1.3 %dynamic_slice.41 = s32[1]{0:T(128)} dynamic-slice(s32[16]{0:T(128)} %get-tuple-element.227, s32[]{:T(128)S(6)} %copy.10), dynamic_slice_sizes={1} | dynamic-slice | bytes 12 | tf_op jit(solution)/shard_map/while/body/eval_jaxpr/dynamic_slice | solution.py:63
  44.6 1.3 %dynamic_slice.41 = s32[1]{0:T(128)} dynamic-slice(s32[16]{0:T(128)} %get-tuple-element.227, s32[]{:T(128)S(6)} %copy.10), dynamic_slice_sizes={1} | dynamic-slice | bytes 12 | tf_op jit(solution)/shard_map/while/body/eval_jaxpr/dynamic_slice | solution.py:63
  47.7 1.3 %dynamic_slice.41 = s32[1]{0:T(128)} dynamic-slice(s32[16]{0:T(128)} %get-tuple-element.227, s32[]{:T(128)S(6)} %copy.10), dynamic_slice_sizes={1} | dynamic-slice | bytes 12 | tf_op jit(solution)/shard_map/while/body/eval_jaxpr/dynamic_slice | solution.py:63
  50.8 1.3 %dynamic_slice.41 = s32[1]{0:T(128)} dynamic-slice(s32[16]{0:T(128)} %get-tuple-element.227, s32[]{:T(128)S(6)} %copy.10), dynamic_slice_sizes={1} | dynamic-slice | bytes 12 | tf_op jit(solution)/shard_map/while/body/eval_jaxpr/dynamic_slice | solution.py:63
  53.9 1.3 %dynamic_slice.41 = s32[1]{0:T(128)} dynamic-slice(s32[16]{0:T(128)} %get-tuple-element.227, s32[]{:T(128)S(6)} %copy.10), dynamic_slice_sizes={1} | dynamic-slice | bytes 12 | tf_op jit(solution)/shard_map/while/body/eval_jaxpr/dynamic_slice | solution.py:63
  57.0 1.3 %dynamic_slice.41 = s32[1]{0:T(128)} dynamic-slice(s32[16]{0:T(128)} %get-tuple-element.227, s32[]{:T(128)S(6)} %copy.10), dynamic_slice_sizes={1} | dynamic-slice | bytes 12 | tf_op jit(solution)/shard_map/while/body/eval_jaxpr/dynamic_slice | solution.py:63
  60.2 1.3 %dynamic_slice.41 = s32[1]{0:T(128)} dynamic-slice(s32[16]{0:T(128)} %get-tuple-element.227, s32[]{:T(128)S(6)} %copy.10), dynamic_slice_sizes={1} | dynamic-slice | bytes 12 | tf_op jit(solution)/shard_map/while/body/eval_jaxpr/dynamic_slice | solution.py:63
  63.3 1.3 %dynamic_slice.41 = s32[1]{0:T(128)} dynamic-slice(s32[16]{0:T(128)} %get-tuple-element.227, s32[]{:T(128)S(6)} %copy.10), dynamic_slice_sizes={1} | dynamic-slice | bytes 12 | tf_op jit(solution)/shard_map/while/body/eval_jaxpr/dynamic_slice | solution.py:63
  66.4 1.3 %dynamic_slice.41 = s32[1]{0:T(128)} dynamic-slice(s32[16]{0:T(128)} %get-tuple-element.227, s32[]{:T(128)S(6)} %copy.10), dynamic_slice_sizes={1} | dynamic-slice | bytes 12 | tf_op jit(solution)/shard_map/while/body/eval_jaxpr/dynamic_slice | solution.py:63
  69.5 1.3 %dynamic_slice.41 = s32[1]{0:T(128)} dynamic-slice(s32[16]{0:T(128)} %get-tuple-element.227, s32[]{:T(128)S(6)} %copy.10), dynamic_slice_sizes={1} | dynamic-slice | bytes 12 | tf_op jit(solution)/shard_map/while/body/eval_jaxpr/dynamic_slice | solution.py:63
  73.5 1.3 %collective-permute-start = (f32[4,16,256]{2,1,0:T(8,128)S(1)}, f32[4,16,256]{2,1,0:T(8,128)S(1)}, u32[]{:S(2)}, u32[]{:S(2)}) collective-permute-start(f32[4,16,256]{2,1,0:T(8,128)S(1)} %get-tuple-element.171), channel_id=1, source_target_pairs={{4,0},{8,4},{12,8},{5,1},{9,5},{13,9},{6,2},{10,6},{14,10},{7,3},{... | collective-permute-start | bytes 196616 | tf_op jit(solution)/shard_map/ppermute | solution.py:20
  74.8 4.5 %collective-permute-start.1 = (f32[4,16,256]{2,1,0:T(8,128)S(1)}, f32[4,16,256]{2,1,0:T(8,128)S(1)}, u32[]{:S(2)}, u32[]{:S(2)}) collective-permute-start(f32[4,16,256]{2,1,0:T(8,128)S(1)} %get-tuple-element.172), channel_id=1, source_target_pairs={{0,4},{4,8},{8,12},{1,5},{5,9},{9,13},{2,6},{6,10},{10,14},{3,7},{... | collective-permute-start | bytes 196616 | tf_op jit(solution)/shard_map/ppermute | solution.py:18
  79.6 1.6 %collective-permute-done.1 = f32[4,16,256]{2,1,0:T(8,128)S(1)} collective-permute-done((f32[4,16,256]{2,1,0:T(8,128)S(1)}, f32[4,16,256]{2,1,0:T(8,128)S(1)}, u32[]{:S(2)}, u32[]{:S(2)}) %collective-permute-start.1) | collective-permute-done | bytes 65568 | tf_op jit(solution)/shard_map/ppermute | solution.py:18
  81.3 3.4 %collective-permute-start.3 = (f32[16,4,256]{2,1,0:T(4,128)S(1)}, f32[16,4,256]{2,1,0:T(4,128)S(1)}, u32[]{:S(2)}, u32[]{:S(2)}) collective-permute-start(f32[16,4,256]{2,1,0:T(4,128)S(1)} %get-tuple-element.169), channel_id=1, source_target_pairs={{0,2},{1,3},{4,6},{5,7},{8,10},{9,11},{12,14},{13,15},{16,18},{17,... | collective-permute-start | bytes 196616 | tf_op jit(solution)/shard_map/ppermute | solution.py:18
  84.7 1.3 %collective-permute-start.2 = (f32[16,4,256]{2,1,0:T(4,128)S(1)}, f32[16,4,256]{2,1,0:T(4,128)S(1)}, u32[]{:S(2)}, u32[]{:S(2)}) collective-permute-start(f32[16,4,256]{2,1,0:T(4,128)S(1)} %get-tuple-element.170), channel_id=1, source_target_pairs={{2,0},{3,1},{6,4},{7,5},{10,8},{11,9},{14,12},{15,13},{18,16},{19,... | collective-permute-start | bytes 196616 | tf_op jit(solution)/shard_map/ppermute | solution.py:20
  86.5 4.3 %collective-permute-done.2 = f32[16,4,256]{2,1,0:T(4,128)S(1)} collective-permute-done((f32[16,4,256]{2,1,0:T(4,128)S(1)}, f32[16,4,256]{2,1,0:T(4,128)S(1)}, u32[]{:S(2)}, u32[]{:S(2)}) %collective-permute-start.2) | collective-permute-done | bytes 65568 | tf_op jit(solution)/shard_map/ppermute | solution.py:20
  91.2 5.8 %reduce-scatter.2.cloned.1.call-done = f32[8,16,256]{2,1,0:T(8,128)} async-done(((f32[32,16,256]{2,1,0:T(8,128)}), f32[8,16,256]{2,1,0:T(8,128)}) %reduce-scatter.2.cloned.1.call-update) | async-done | bytes 131088 | tf_op jit(solution)/shard_map/reduce_scatter | solution.py:71
  97.0 1.9 %fusion.14 = f32[1,8,16,256]{3,2,1,0:T(8,128)} fusion(f32[8,16,256]{2,1,0:T(8,128)S(1)} %copy-done.2, f32[8,16,256]{2,1,0:T(8,128)} %reduce-scatter.2.cloned.1.call-done, f32[8,16,256]{2,1,0:T(8,128)S(1)} %bitcast.27, f32[4,16,256]{2,1,0:T(8,128)S(1)} %collective-permute-done.1, f32[4,16,256]{2,1,0:T(8,128)S(1)} %collective-permute-done, ...), kind=kLoop, calls=%fused_computation.35 | loop fusion | flops 1376256 | bytes 2883584 | tf_op jit(solution)/shard_map/broadcast_in_dim | solution.py:85
  (28 shorter events, 14.2 us)
Async XLA Ops:
  6.5 90.5 %reduce-scatter.2.cloned.1.call-start = ((), (), s32[]{:S(2)}) async-start(), calls=%async_computation.1 | async-start | bytes 655360 | tf_op jit(solution)/shard_map/reduce_scatter | solution.py:71
  22.6 50.8 %copy-start.1 = (f32[1,8,16,256]{3,2,1,0:T(8,128)S(1)}, f32[1,8,16,256]{3,2,1,0:T(8,128)}, u32[]{:S(2)}) copy-start(f32[1,8,16,256]{3,2,1,0:T(8,128)} %param.11) | copy-start | bytes 393220
  22.6 74.4 %copy-start.2 = (f32[8,16,256]{2,1,0:T(8,128)S(1)}, f32[8,16,256]{2,1,0:T(8,128)}, u32[]{:S(2)}) copy-start(f32[8,16,256]{2,1,0:T(8,128)} %param.13) | copy-start | bytes 393220
  22.6 74.4 %copy-start.3 = (f32[1,8,16,256]{3,2,1,0:T(8,128)S(1)}, f32[1,8,16,256]{3,2,1,0:T(8,128)}, u32[]{:S(2)}) copy-start(f32[1,8,16,256]{3,2,1,0:T(8,128)} %param.12) | copy-start | bytes 393220
  72.6 0.8 copy-start
  73.5 6.2 %collective-permute-start = (f32[4,16,256]{2,1,0:T(8,128)S(1)}, f32[4,16,256]{2,1,0:T(8,128)S(1)}, u32[]{:S(2)}, u32[]{:S(2)}) collective-permute-start(f32[4,16,256]{2,1,0:T(8,128)S(1)} %get-tuple-element.171), channel_id=1, source_target_pairs={{4,0},{8,4},{12,8},{5,1},{9,5},{13,9},{6,2},{10,6},{14,10},{7,3},{... | collective-permute-start | bytes 196616 | tf_op jit(solution)/shard_map/ppermute | solution.py:20
  74.8 6.5 %collective-permute-start.1 = (f32[4,16,256]{2,1,0:T(8,128)S(1)}, f32[4,16,256]{2,1,0:T(8,128)S(1)}, u32[]{:S(2)}, u32[]{:S(2)}) collective-permute-start(f32[4,16,256]{2,1,0:T(8,128)S(1)} %get-tuple-element.172), channel_id=1, source_target_pairs={{0,4},{4,8},{8,12},{1,5},{5,9},{9,13},{2,6},{6,10},{10,14},{3,7},{... | collective-permute-start | bytes 196616 | tf_op jit(solution)/shard_map/ppermute | solution.py:18
  81.3 5.3 %collective-permute-start.3 = (f32[16,4,256]{2,1,0:T(4,128)S(1)}, f32[16,4,256]{2,1,0:T(4,128)S(1)}, u32[]{:S(2)}, u32[]{:S(2)}) collective-permute-start(f32[16,4,256]{2,1,0:T(4,128)S(1)} %get-tuple-element.169), channel_id=1, source_target_pairs={{0,2},{1,3},{4,6},{5,7},{8,10},{9,11},{12,14},{13,15},{16,18},{17,... | collective-permute-start | bytes 196616 | tf_op jit(solution)/shard_map/ppermute | solution.py:18
  84.7 6.2 %collective-permute-start.2 = (f32[16,4,256]{2,1,0:T(4,128)S(1)}, f32[16,4,256]{2,1,0:T(4,128)S(1)}, u32[]{:S(2)}, u32[]{:S(2)}) collective-permute-start(f32[16,4,256]{2,1,0:T(4,128)S(1)} %get-tuple-element.170), channel_id=1, source_target_pairs={{2,0},{3,1},{6,4},{7,5},{10,8},{11,9},{14,12},{15,13},{18,16},{19,... | collective-permute-start | bytes 196616 | tf_op jit(solution)/shard_map/ppermute | solution.py:20
Sparse Core Ops, SparseCore 0:
  73.6 23.3 reduce-scatter.1
where the time goes:
time: 107 us; the launch traced here: 106 us
  other arithmetic  21.3 us (20%)
  local copies, waits for them, and re-layouts  21.3 us (20%)
  blocking collectives  15.9 us (15%)
  between operations  13.5 us (13%)
  waiting for transfers between devices  12.6 us (12%)
  loops' own time  10.6 us (10%)
  starting transfers between devices  10.5 us (10%)
    dynamic_slice x16, local copies, waits for them, and re-layouts, add_column(): offset_cells = offset_of[column] - half_span  20.3 us
    add x16, other arithmetic, add_column(): return running + whole_col.astype(jnp.float32) * shifted.astype(jnp.float32)  19 us
    all_gather x1, blocking collectives, on_device(): gathered = lax.all_gather(background, 'off', axis=1, tiled=True)  15.9 us
    another operation x1, loops' own time, on_device(): lax.fori_loop(0, local_cols, add_column, jnp.zeros((slab_rows * lax.axis_...  10.6 us
    ppermute x2, starting transfers between devices, extended_2(): lax.ppermute(tail, axis, [(i, (i + 1) % count) for i in range(ends)])  7.91 us
    reduce_scatter x1, waiting for transfers between devices, on_device(): lax.psum_scatter(lax.fori_loop(0, local_cols, add_column, jnp.zeros((slab...  5.78 us
    ppermute x2, waiting for transfers between devices, extended_2(): lax.ppermute(head, axis, [((i + 1) % count, i) for i in range(ends)])  4.58 us
    ppermute x2, starting transfers between devices, extended_2(): lax.ppermute(head, axis, [((i + 1) % count, i) for i in range(ends)])  2.58 us
  transfers between devices with their start and end apart: 5, of which 5 were waited for; matrix products, arithmetic and copies ran while one was open for 0% of the time, Pallas kernels for 0%

commit v1 on v0

--- a/solution.py
+++ b/solution.py
@@ -55,7 +55,12 @@
     width_x = wave_now.shape[3]
     local_cols = image.shape[0]
     half_span = H // 2
-    gathered = lax.all_gather(background, "off", axis=1, tiled=True)
+    ring = [background]
+    for hop in range(3):
+        ring.append(lax.ppermute(ring[-1], "off", [(dev, (dev + 1) % 4) for dev in range(4)]))
+    gathered = jnp.roll(
+        jnp.concatenate(ring[::-1], axis=1), (lax.axis_index("off") + 1) * ring[0].shape[1], axis=1
+    )
     extended_bg = jnp.pad(gathered[0], ((0, 0), (0, 0), (half_span, half_span)))
     first_index = jnp.asarray(jnp.int32(0), jnp.int32)
 

time: 107 us -> 110 us (1.028)
  blocking collectives: 15.9 us -> 0 us
  waiting for transfers between devices: 12.6 us -> 24.8 us
  starting transfers between devices: 10.5 us -> 14.7 us
  local copies, waits for them, and re-layouts: 21.3 us -> 23.7 us
    ppermute x0 -> x3, waiting for transfers between devices: none -> 16.6 us  [on_device(): lax.ppermute(ring[-1], 'off', [(dev, (dev + 1) % 4) for dev in range(4)])]
    all_gather x1 -> x0, blocking collectives: 15.9 us -> none  [on_device(): gathered = lax.all_gather(background, 'off', axis=1, tiled=True)]
    ppermute x2, waiting for transfers between devices: 4.58 us -> 0.61 us  [extended_2(): lax.ppermute(head, axis, [((i + 1) % count, i) for i in range(ends)])]
    ppermute x0 -> x3, starting transfers between devices: none -> 3.06 us  [on_device(): lax.ppermute(ring[-1], 'off', [(dev, (dev + 1) % 4) for dev in range(4)])]
    reduce_scatter x1, waiting for transfers between devices: 5.78 us -> 4.34 us  [on_device(): lax.psum_scatter(lax.fori_loop(0, local_cols, add_column, jnp.zeros((slab...]
    ppermute x2, starting transfers between devices: 7.91 us -> 9.1 us  [extended_2(): lax.ppermute(tail, axis, [(i, (i + 1) % count) for i in range(ends)])]
  transfers between devices with their start and end apart: 5 -> 8, of which waited for: 5 -> 8; matrix products, arithmetic and copies ran while one was open for 0% -> 0% of each run, Pallas kernels for 0% -> 0%
where the time goes in v1:
time: 110 us; the launch traced here: 109 us
  waiting for transfers between devices  24.8 us (23%)
  local copies, waits for them, and re-layouts  23.7 us (22%)
  other arithmetic  21.3 us (19%)
  starting transfers between devices  14.7 us (13%)
  between operations  13.5 us (12%)
  loops' own time  10.4 us (9%)
    dynamic_slice x16, local copies, waits for them, and re-layouts, add_column(): offset_cells = offset_of[column] - half_span  20.9 us
    add x16, other arithmetic, add_column(): return running + whole_col.astype(jnp.float32) * shifted.astype(jnp.float32)  19 us
    ppermute x3, waiting for transfers between devices, on_device(): lax.ppermute(ring[-1], 'off', [(dev, (dev + 1) % 4) for dev in range(4)])  16.6 us
    another operation x1, loops' own time, on_device(): lax.fori_loop(0, local_cols, add_column, jnp.zeros((slab_rows * lax.axis_...  10.4 us
    ppermute x2, starting transfers between devices, extended_2(): lax.ppermute(tail, axis, [(i, (i + 1) % count) for i in range(ends)])  9.1 us
    reduce_scatter x1, waiting for transfers between devices, on_device(): lax.psum_scatter(lax.fori_loop(0, local_cols, add_column, jnp.zeros((slab...  4.34 us
    ppermute x2, waiting for transfers between devices, extended_2(): lax.ppermute(tail, axis, [(i, (i + 1) % count) for i in range(ends)])  3.28 us
    ppermute x3, starting transfers between devices, on_device(): lax.ppermute(ring[-1], 'off', [(dev, (dev + 1) % 4) for dev in range(4)])  3.06 us
  transfers between devices with their start and end apart: 8, of which 8 were waited for; matrix products, arithmetic and copies ran while one was open for 0% of the time, Pallas kernels for 0%

profile of v1, /device:TPU:0, one launch (start us, length us, event | category | flops | bytes accessed | tf_op | source)
XLA Modules:
  0.0 108.5 jit_solution(14719529503544608043)
XLA Ops:
  6.5 3.1 %collective-permute-start.4 = (bf16[1,8,16,256]{3,2,1,0:T(8,128)(2,1)}, bf16[1,8,16,256]{3,2,1,0:T(8,128)(2,1)S(1)}, u32[]{:S(2)}, u32[]{:S(2)}) collective-permute-start(bf16[1,8,16,256]{3,2,1,0:T(8,128)(2,1)} %param.10), channel_id=1, source_target_pairs={{0,4},{4,8},{8,12},{12,0},{1,5},{5,9},{9,13},{13,1},{2,6},{6,10},{... | collective-permute-start | bytes 196616 | tf_op jit(solution)/shard_map/ppermute | solution.py:60
  9.6 4.5 %collective-permute-done.4 = bf16[1,8,16,256]{3,2,1,0:T(8,128)(2,1)S(1)} collective-permute-done((bf16[1,8,16,256]{3,2,1,0:T(8,128)(2,1)}, bf16[1,8,16,256]{3,2,1,0:T(8,128)(2,1)S(1)}, u32[]{:S(2)}, u32[]{:S(2)}) %collective-permute-start.4) | collective-permute-done | bytes 65568 | tf_op jit(solution)/shard_map/ppermute | solution.py:60
  14.1 6.1 %collective-permute-done.5 = bf16[1,8,16,256]{3,2,1,0:T(8,128)(2,1)S(1)} collective-permute-done((bf16[1,8,16,256]{3,2,1,0:T(8,128)(2,1)S(1)}, bf16[1,8,16,256]{3,2,1,0:T(8,128)(2,1)S(1)}, u32[]{:S(2)}, u32[]{:S(2)}) %collective-permute-start.5) | collective-permute-done | bytes 65568 | tf_op jit(solution)/shard_map/ppermute | solution.py:60
  20.1 6.1 %collective-permute-done.6 = bf16[1,8,16,256]{3,2,1,0:T(8,128)(2,1)S(1)} collective-permute-done((bf16[1,8,16,256]{3,2,1,0:T(8,128)(2,1)S(1)}, bf16[1,8,16,256]{3,2,1,0:T(8,128)(2,1)S(1)}, u32[]{:S(2)}, u32[]{:S(2)}) %collective-permute-start.6) | collective-permute-done | bytes 65568 | tf_op jit(solution)/shard_map/ppermute | solution.py:60
  28.2 50.4 %while.16 = (s32[]{:T(128)}, f32[32,16,256]{2,1,0:T(8,128)S(1)}, bf16[16,32,16,256]{3,2,1,0:T(8,128)(2,1)}, s32[16]{0:T(128)}, bf16[32,16,320]{2,1,0:T(8,128)(2,...) while((s32[]{:T(128)}, f32[32,16,256]{2,1,0:T(8,128)S(1)}, ...), condition=%wide.region_1.2_spmd.clone, body=%wide.region_0.1_spmd.clone.sunk | while | flops 655368 | bytes 1573053 | solution.py:77
  28.2 1.4 %dynamic_slice.47 = s32[1]{0:T(128)} dynamic-slice(s32[16]{0:T(128)} %get-tuple-element.227, s32[]{:T(128)} %get-tuple-element.214), dynamic_slice_sizes={1} | dynamic-slice | bytes 12 | tf_op jit(solution)/shard_map/while/body/eval_jaxpr/dynamic_slice | solution.py:68
  30.3 1.2 %fusion.37 = f32[32,16,256]{2,1,0:T(8,128)S(1)} fusion(f32[32,16,256]{2,1,0:T(8,128)S(1)} %get-tuple-element.215, bf16[32,16,320]{2,1,0:T(8,128)(2,1)S(1)} %get-tuple-element.228, s32[]{:T(128)S(6)} %select_n.37, bf16[16,32,16,256]{3,2,1,0:T(8,128)(2,1)} %get-tuple-element.226, s32[]{:T(128)} %get-tuple-element.214, pred[]{:T(512)S(6)} %compare.24), kind=kLoop, calls=%fused_computation.1.clone.1 | loop fusion | flops 655360 | bytes 1572873 | tf_op jit(solution)/shard_map/while/body/eval_jaxpr/add | solution.py:74
  31.5 1.3 %dynamic_slice.47 = s32[1]{0:T(128)} dynamic-slice(s32[16]{0:T(128)} %get-tuple-element.227, s32[]{:T(128)} %get-tuple-element.214), dynamic_slice_sizes={1} | dynamic-slice | bytes 12 | tf_op jit(solution)/shard_map/while/body/eval_jaxpr/dynamic_slice | solution.py:68
  34.6 1.3 %dynamic_slice.47 = s32[1]{0:T(128)} dynamic-slice(s32[16]{0:T(128)} %get-tuple-element.227, s32[]{:T(128)} %get-tuple-element.214), dynamic_slice_sizes={1} | dynamic-slice | bytes 12 | tf_op jit(solution)/shard_map/while/body/eval_jaxpr/dynamic_slice | solution.py:68
  37.7 1.3 %dynamic_slice.47 = s32[1]{0:T(128)} dynamic-slice(s32[16]{0:T(128)} %get-tuple-element.227, s32[]{:T(128)} %get-tuple-element.214), dynamic_slice_sizes={1} | dynamic-slice | bytes 12 | tf_op jit(solution)/shard_map/while/body/eval_jaxpr/dynamic_slice | solution.py:68
  40.9 1.3 %dynamic_slice.47 = s32[1]{0:T(128)} dynamic-slice(s32[16]{0:T(128)} %get-tuple-element.227, s32[]{:T(128)} %get-tuple-element.214), dynamic_slice_sizes={1} | dynamic-slice | bytes 12 | tf_op jit(solution)/shard_map/while/body/eval_jaxpr/dynamic_slice | solution.py:68
  44.0 1.3 %dynamic_slice.47 = s32[1]{0:T(128)} dynamic-slice(s32[16]{0:T(128)} %get-tuple-element.227, s32[]{:T(128)} %get-tuple-element.214), dynamic_slice_sizes={1} | dynamic-slice | bytes 12 | tf_op jit(solution)/shard_map/while/body/eval_jaxpr/dynamic_slice | solution.py:68
  47.2 1.3 %dynamic_slice.47 = s32[1]{0:T(128)} dynamic-slice(s32[16]{0:T(128)} %get-tuple-element.227, s32[]{:T(128)} %get-tuple-element.214), dynamic_slice_sizes={1} | dynamic-slice | bytes 12 | tf_op jit(solution)/shard_map/while/body/eval_jaxpr/dynamic_slice | solution.py:68
  49.1 1.2 %fusion.37 = f32[32,16,256]{2,1,0:T(8,128)S(1)} fusion(f32[32,16,256]{2,1,0:T(8,128)S(1)} %get-tuple-element.215, bf16[32,16,320]{2,1,0:T(8,128)(2,1)S(1)} %get-tuple-element.228, s32[]{:T(128)S(6)} %select_n.37, bf16[16,32,16,256]{3,2,1,0:T(8,128)(2,1)} %get-tuple-element.226, s32[]{:T(128)} %get-tuple-element.214, pred[]{:T(512)S(6)} %compare.24), kind=kLoop, calls=%fused_computation.1.clone.1 | loop fusion | flops 655360 | bytes 1572873 | tf_op jit(solution)/shard_map/while/body/eval_jaxpr/add | solution.py:74
  50.3 1.3 %dynamic_slice.47 = s32[1]{0:T(128)} dynamic-slice(s32[16]{0:T(128)} %get-tuple-element.227, s32[]{:T(128)} %get-tuple-element.214), dynamic_slice_sizes={1} | dynamic-slice | bytes 12 | tf_op jit(solution)/shard_map/while/body/eval_jaxpr/dynamic_slice | solution.py:68
  52.3 1.2 %fusion.37 = f32[32,16,256]{2,1,0:T(8,128)S(1)} fusion(f32[32,16,256]{2,1,0:T(8,128)S(1)} %get-tuple-element.215, bf16[32,16,320]{2,1,0:T(8,128)(2,1)S(1)} %get-tuple-element.228, s32[]{:T(128)S(6)} %select_n.37, bf16[16,32,16,256]{3,2,1,0:T(8,128)(2,1)} %get-tuple-element.226, s32[]{:T(128)} %get-tuple-element.214, pred[]{:T(512)S(6)} %compare.24), kind=kLoop, calls=%fused_computation.1.clone.1 | loop fusion | flops 655360 | bytes 1572873 | tf_op jit(solution)/shard_map/while/body/eval_jaxpr/add | solution.py:74
  53.5 1.3 %dynamic_slice.47 = s32[1]{0:T(128)} dynamic-slice(s32[16]{0:T(128)} %get-tuple-element.227, s32[]{:T(128)} %get-tuple-element.214), dynamic_slice_sizes={1} | dynamic-slice | bytes 12 | tf_op jit(solution)/shard_map/while/body/eval_jaxpr/dynamic_slice | solution.py:68
  56.6 1.3 %dynamic_slice.47 = s32[1]{0:T(128)} dynamic-slice(s32[16]{0:T(128)} %get-tuple-element.227, s32[]{:T(128)} %get-tuple-element.214), dynamic_slice_sizes={1} | dynamic-slice | bytes 12 | tf_op jit(solution)/shard_map/while/body/eval_jaxpr/dynamic_slice | solution.py:68
  59.7 1.3 %dynamic_slice.47 = s32[1]{0:T(128)} dynamic-slice(s32[16]{0:T(128)} %get-tuple-element.227, s32[]{:T(128)} %get-tuple-element.214), dynamic_slice_sizes={1} | dynamic-slice | bytes 12 | tf_op jit(solution)/shard_map/while/body/eval_jaxpr/dynamic_slice | solution.py:68
  62.9 1.3 %dynamic_slice.47 = s32[1]{0:T(128)} dynamic-slice(s32[16]{0:T(128)} %get-tuple-element.227, s32[]{:T(128)} %get-tuple-element.214), dynamic_slice_sizes={1} | dynamic-slice | bytes 12 | tf_op jit(solution)/shard_map/while/body/eval_jaxpr/dynamic_slice | solution.py:68
  66.0 1.3 %dynamic_slice.47 = s32[1]{0:T(128)} dynamic-slice(s32[16]{0:T(128)} %get-tuple-element.227, s32[]{:T(128)} %get-tuple-element.214), dynamic_slice_sizes={1} | dynamic-slice | bytes 12 | tf_op jit(solution)/shard_map/while/body/eval_jaxpr/dynamic_slice | solution.py:68
  69.2 1.3 %dynamic_slice.47 = s32[1]{0:T(128)} dynamic-slice(s32[16]{0:T(128)} %get-tuple-element.227, s32[]{:T(128)} %get-tuple-element.214), dynamic_slice_sizes={1} | dynamic-slice | bytes 12 | tf_op jit(solution)/shard_map/while/body/eval_jaxpr/dynamic_slice | solution.py:68
  72.3 1.3 %dynamic_slice.47 = s32[1]{0:T(128)} dynamic-slice(s32[16]{0:T(128)} %get-tuple-element.227, s32[]{:T(128)} %get-tuple-element.214), dynamic_slice_sizes={1} | dynamic-slice | bytes 12 | tf_op jit(solution)/shard_map/while/body/eval_jaxpr/dynamic_slice | solution.py:68
  75.5 1.3 %dynamic_slice.47 = s32[1]{0:T(128)} dynamic-slice(s32[16]{0:T(128)} %get-tuple-element.227, s32[]{:T(128)} %get-tuple-element.214), dynamic_slice_sizes={1} | dynamic-slice | bytes 12 | tf_op jit(solution)/shard_map/while/body/eval_jaxpr/dynamic_slice | solution.py:68
  79.4 1.3 %collective-permute-start = (f32[4,16,256]{2,1,0:T(8,128)S(1)}, f32[4,16,256]{2,1,0:T(8,128)S(1)}, u32[]{:S(2)}, u32[]{:S(2)}) collective-permute-start(f32[4,16,256]{2,1,0:T(8,128)S(1)} %get-tuple-element.171), channel_id=1, source_target_pairs={{4,0},{8,4},{12,8},{5,1},{9,5},{13,9},{6,2},{10,6},{14,10},{7,3},{... | collective-permute-start | bytes 196616 | tf_op jit(solution)/shard_map/ppermute | solution.py:20
  80.7 4.5 %collective-permute-start.1 = (f32[4,16,256]{2,1,0:T(8,128)S(1)}, f32[4,16,256]{2,1,0:T(8,128)S(1)}, u32[]{:S(2)}, u32[]{:S(2)}) collective-permute-start(f32[4,16,256]{2,1,0:T(8,128)S(1)} %get-tuple-element.172), channel_id=1, source_target_pairs={{0,4},{4,8},{8,12},{1,5},{5,9},{9,13},{2,6},{6,10},{10,14},{3,7},{... | collective-permute-start | bytes 196616 | tf_op jit(solution)/shard_map/ppermute | solution.py:18
  85.6 1.7 %collective-permute-done.1 = f32[4,16,256]{2,1,0:T(8,128)S(1)} collective-permute-done((f32[4,16,256]{2,1,0:T(8,128)S(1)}, f32[4,16,256]{2,1,0:T(8,128)S(1)}, u32[]{:S(2)}, u32[]{:S(2)}) %collective-permute-start.1) | collective-permute-done | bytes 65568 | tf_op jit(solution)/shard_map/ppermute | solution.py:18
  87.3 1.3 %collective-permute-start.2 = (f32[16,4,256]{2,1,0:T(4,128)S(1)}, f32[16,4,256]{2,1,0:T(4,128)S(1)}, u32[]{:S(2)}, u32[]{:S(2)}) collective-permute-start(f32[16,4,256]{2,1,0:T(4,128)S(1)} %get-tuple-element.170), channel_id=1, source_target_pairs={{2,0},{3,1},{6,4},{7,5},{10,8},{11,9},{14,12},{15,13},{18,16},{19,... | collective-permute-start | bytes 196616 | tf_op jit(solution)/shard_map/ppermute | solution.py:20
  88.6 4.5 %collective-permute-start.3 = (f32[16,4,256]{2,1,0:T(4,128)S(1)}, f32[16,4,256]{2,1,0:T(4,128)S(1)}, u32[]{:S(2)}, u32[]{:S(2)}) collective-permute-start(f32[16,4,256]{2,1,0:T(4,128)S(1)} %get-tuple-element.169), channel_id=1, source_target_pairs={{0,2},{1,3},{4,6},{5,7},{8,10},{9,11},{12,14},{13,15},{16,18},{17,... | collective-permute-start | bytes 196616 | tf_op jit(solution)/shard_map/ppermute | solution.py:18
  93.5 1.6 %collective-permute-done.3 = f32[16,4,256]{2,1,0:T(4,128)S(1)} collective-permute-done((f32[16,4,256]{2,1,0:T(4,128)S(1)}, f32[16,4,256]{2,1,0:T(4,128)S(1)}, u32[]{:S(2)}, u32[]{:S(2)}) %collective-permute-start.3) | collective-permute-done | bytes 65568 | tf_op jit(solution)/shard_map/ppermute | solution.py:18
  95.5 4.3 %reduce-scatter.2.cloned.1.call-done = f32[8,16,256]{2,1,0:T(8,128)} async-done(((f32[32,16,256]{2,1,0:T(8,128)}), f32[8,16,256]{2,1,0:T(8,128)}) %reduce-scatter.2.cloned.1.call-update) | async-done | bytes 131088 | tf_op jit(solution)/shard_map/reduce_scatter | solution.py:76
  99.8 1.9 %fusion.14 = f32[1,8,16,256]{3,2,1,0:T(8,128)} fusion(f32[8,16,256]{2,1,0:T(8,128)S(1)} %copy-done.2, f32[8,16,256]{2,1,0:T(8,128)} %reduce-scatter.2.cloned.1.call-done, f32[8,16,256]{2,1,0:T(8,128)S(1)} %bitcast.27, f32[4,16,256]{2,1,0:T(8,128)S(1)} %collective-permute-done.1, f32[4,16,256]{2,1,0:T(8,128)S(1)} %collective-permute-done, ...), kind=kLoop, calls=%fused_computation.36 | loop fusion | flops 1376256 | bytes 2883584 | tf_op jit(solution)/shard_map/broadcast_in_dim | solution.py:90
  (42 shorter events, 19.2 us)
Async XLA Ops:
  6.5 93.3 %reduce-scatter.2.cloned.1.call-start = ((), (), s32[]{:S(2)}) async-start(), calls=%async_computation.1 | async-start | bytes 655360 | tf_op jit(solution)/shard_map/reduce_scatter | solution.py:76
  6.5 7.5 %collective-permute-start.4 = (bf16[1,8,16,256]{3,2,1,0:T(8,128)(2,1)}, bf16[1,8,16,256]{3,2,1,0:T(8,128)(2,1)S(1)}, u32[]{:S(2)}, u32[]{:S(2)}) collective-permute-start(bf16[1,8,16,256]{3,2,1,0:T(8,128)(2,1)} %param.10), channel_id=1, source_target_pairs={{0,4},{4,8},{8,12},{12,0},{1,5},{5,9},{9,13},{13,1},{2,6},{6,10},{... | collective-permute-start | bytes 196616 | tf_op jit(solution)/shard_map/ppermute | solution.py:60
  14.1 6.1 %collective-permute-start.5 = (bf16[1,8,16,256]{3,2,1,0:T(8,128)(2,1)S(1)}, bf16[1,8,16,256]{3,2,1,0:T(8,128)(2,1)S(1)}, u32[]{:S(2)}, u32[]{:S(2)}) collective-permute-start(bf16[1,8,16,256]{3,2,1,0:T(8,128)(2,1)S(1)} %collective-permute-done.4), channel_id=1, source_target_pairs={{0,4},{4,8},{8,12},{12,0},{1,5},{5,9},{9,13},{13,1},{2,6},{6,10},{... | collective-permute-start | bytes 196616 | tf_op jit(solution)/shard_map/ppermute | solution.py:60
  20.1 6.1 %collective-permute-start.6 = (bf16[1,8,16,256]{3,2,1,0:T(8,128)(2,1)S(1)}, bf16[1,8,16,256]{3,2,1,0:T(8,128)(2,1)S(1)}, u32[]{:S(2)}, u32[]{:S(2)}) collective-permute-start(bf16[1,8,16,256]{3,2,1,0:T(8,128)(2,1)S(1)} %collective-permute-done.5), channel_id=1, source_target_pairs={{0,4},{4,8},{8,12},{12,0},{1,5},{5,9},{9,13},{13,1},{2,6},{6,10},{... | collective-permute-start | bytes 196616 | tf_op jit(solution)/shard_map/ppermute | solution.py:60
  28.2 51.2 %copy-start.1 = (f32[1,8,16,256]{3,2,1,0:T(8,128)S(1)}, f32[1,8,16,256]{3,2,1,0:T(8,128)}, u32[]{:S(2)}) copy-start(f32[1,8,16,256]{3,2,1,0:T(8,128)} %param.11) | copy-start | bytes 393220
  28.2 71.6 %copy-start.2 = (f32[8,16,256]{2,1,0:T(8,128)S(1)}, f32[8,16,256]{2,1,0:T(8,128)}, u32[]{:S(2)}) copy-start(f32[8,16,256]{2,1,0:T(8,128)} %param.13) | copy-start | bytes 393220
  28.2 71.6 %copy-start.3 = (f32[1,8,16,256]{3,2,1,0:T(8,128)S(1)}, f32[1,8,16,256]{3,2,1,0:T(8,128)}, u32[]{:S(2)}) copy-start(f32[1,8,16,256]{3,2,1,0:T(8,128)} %param.12) | copy-start | bytes 393220
  78.6 0.8 copy-start
  79.4 6.2 %collective-permute-start = (f32[4,16,256]{2,1,0:T(8,128)S(1)}, f32[4,16,256]{2,1,0:T(8,128)S(1)}, u32[]{:S(2)}, u32[]{:S(2)}) collective-permute-start(f32[4,16,256]{2,1,0:T(8,128)S(1)} %get-tuple-element.171), channel_id=1, source_target_pairs={{4,0},{8,4},{12,8},{5,1},{9,5},{13,9},{6,2},{10,6},{14,10},{7,3},{... | collective-permute-start | bytes 196616 | tf_op jit(solution)/shard_map/ppermute | solution.py:20
  80.7 6.6 %collective-permute-start.1 = (f32[4,16,256]{2,1,0:T(8,128)S(1)}, f32[4,16,256]{2,1,0:T(8,128)S(1)}, u32[]{:S(2)}, u32[]{:S(2)}) collective-permute-start(f32[4,16,256]{2,1,0:T(8,128)S(1)} %get-tuple-element.172), channel_id=1, source_target_pairs={{0,4},{4,8},{8,12},{1,5},{5,9},{9,13},{2,6},{6,10},{10,14},{3,7},{... | collective-permute-start | bytes 196616 | tf_op jit(solution)/shard_map/ppermute | solution.py:18
  87.3 6.2 %collective-permute-start.2 = (f32[16,4,256]{2,1,0:T(4,128)S(1)}, f32[16,4,256]{2,1,0:T(4,128)S(1)}, u32[]{:S(2)}, u32[]{:S(2)}) collective-permute-start(f32[16,4,256]{2,1,0:T(4,128)S(1)} %get-tuple-element.170), channel_id=1, source_target_pairs={{2,0},{3,1},{6,4},{7,5},{10,8},{11,9},{14,12},{15,13},{18,16},{19,... | collective-permute-start | bytes 196616 | tf_op jit(solution)/shard_map/ppermute | solution.py:20
  88.6 6.4 %collective-permute-start.3 = (f32[16,4,256]{2,1,0:T(4,128)S(1)}, f32[16,4,256]{2,1,0:T(4,128)S(1)}, u32[]{:S(2)}, u32[]{:S(2)}) collective-permute-start(f32[16,4,256]{2,1,0:T(4,128)S(1)} %get-tuple-element.169), channel_id=1, source_target_pairs={{0,2},{1,3},{4,6},{5,7},{8,10},{9,11},{12,14},{13,15},{16,18},{17,... | collective-permute-start | bytes 196616 | tf_op jit(solution)/shard_map/ppermute | solution.py:18
Sparse Core Ops, SparseCore 0:
  79.5 20.2 reduce-scatter.1
